TPU v7x, 32 devices: a whole 2x2x4 slice. The times are simulated.
32 devices in a mesh: src: 4 (over y, core), tgt: 8 (over z, x).
Axes of the slice: x: 2, y: 2, z: 4, core: 2. Of those that a mesh axis runs over, the one named last changes fastest.
Arguments:
- src_vel: bfloat16 [2, 48, 131072], P(None, None, ('src', 'tgt')), may hold values from -6 to 6
- angle: float32 [131072], P(('src', 'tgt')), may hold values from -3.140625 to 3.140625
- src_block: int32 [4, 8, 8, 8], P('src', 'tgt'), may hold values from 0 to 31
- tgt_block: int32 [4, 8, 8, 8], P('src', 'tgt'), may hold values from 0 to 31
- send_count: int32 [4, 8, 8], P('src', 'tgt'), may hold values from 0 to 8, as said below
- intersection: bfloat16 [4, 8, 8, 8, 128, 128], P('src', 'tgt'), may hold values from -0.375 to 0.375
- eofs: bfloat16 [512, 2, 131072], P(None, None, ('src', 'tgt')), may hold values from -0.0234375 to 0.0234375
Outputs:
- remapped: bfloat16 [2, 48, 131072], P(None, None, ('src', 'tgt'))
- pcs: float32 [48, 512], P(None, 'tgt')
Inputs may be any that keep to these rules, and one draw needn't show every extreme that they name: `src_block`: indices of the sending device's own source blocks. `tgt_block`: indices of the receiving device's target blocks. `send_count`: in every tile row, one receiver column gets 8 live slots from every sender of the row.
All inputs are finite; a program needn't handle non-finite values.
Results may differ from a plain program's by a relative error of at most 0.0058.
Values may be sent and summed in bfloat16 or wider, within the bound.
A program may use at most 64 MiB of HBM per device.

v0:
```python
import functools

import jax
import jax.numpy as jnp
from jax import lax
from jax.experimental import pallas as pl
from jax.experimental.pallas import tpu as pltpu
from jax.sharding import PartitionSpec as P

BLK = 128
MESH = pl.DeviceIdType.MESH
NT_DIMS = (((1,), (1,)), ((), ()))


def xor_of(index, mask, count):
    result, bit = 0, 1
    while bit < count:
        result = result + (((index // bit) + (mask // bit)) % 2) * bit
        bit *= 2
    return result


def kernel(
    n, ns, vel_hbm, angle_ref, sblk_ref, tblk_ref, count_ref, w_hbm, eofs_hbm,
    out_hbm, pcs_ref,
    vel, w, eo, flat, mirror, cs, sn, rot, send, recv, ids, rids, kron, rem, res, piece, rpiece, rq,
    vel_sem, w_sem, eo_sem, fold_sem, tx_sem, rx_sem, idtx_sem, idrx_sem, out_sem,
    ptx_sem, prx_sem, qtx_sem, qrx_sem,
):
    s, t = lax.axis_index("src"), lax.axis_index("tgt")
    comps, rows, cells = vel.shape
    sb = cells // BLK
    cap = w.shape[1]
    nt = eo.shape[0]
    tb = rem.shape[1] // BLK
    group = BLK // cap
    both = comps * rows
    order = list(range(n - 1, 0, -1))
    peer = {m: xor_of(t, m, n) for m in range(n)}

    vel_copy = pltpu.make_async_copy(vel_hbm, vel, vel_sem)
    vel_copy.start()
    w_copies = {}
    for k, m in enumerate(order + [0]):
        w_copies[k] = pltpu.make_async_copy(w_hbm.at[xor_of(t, m, n)], w.at[m], w_sem.at[k])
        w_copies[k].start()

    barrier = pltpu.get_barrier_semaphore()
    for m in order:
        pl.semaphore_signal(barrier, inc=1, device_id=(s, peer[m]), device_id_type=MESH)
    for i in range(1, ns):
        pl.semaphore_signal(barrier, inc=1, device_id=((s + i) % ns, t), device_id_type=MESH)

    cs[...] = jnp.cos(angle_ref[...])
    sn[...] = jnp.sin(angle_ref[...])
    lane_slot = lax.broadcasted_iota(jnp.int32, (8, BLK), 1) // group

    def own_ids(p, carry):
        tile = jnp.full((8, BLK), tb, jnp.int32)
        for j in range(cap):
            slot_id = jnp.where(j < count_ref[p], tblk_ref[p, j], tb)
            tile = jnp.where(lane_slot == j, slot_id, tile)
        ids[p] = tile
        return carry

    lax.fori_loop(0, n, own_ids, 0)
    vel_copy.wait()

    def rotate(b, carry):
        lanes = pl.ds(pl.multiple_of(b * BLK, BLK), BLK)
        c, d = cs[pl.ds(b, 1), :], sn[pl.ds(b, 1), :]
        x = vel[0, :, lanes].astype(jnp.float32)
        y = vel[1, :, lanes].astype(jnp.float32)
        rot[b, 0:rows, :] = (c * x - d * y).astype(jnp.bfloat16)
        rot[b, rows:both, :] = (d * x + c * y).astype(jnp.bfloat16)
        return carry

    lax.fori_loop(0, sb, rotate, 0, unroll=2)
    pl.semaphore_wait(barrier, n - 1 + ns - 1)

    def fold_copy():
        return pltpu.make_async_remote_copy(
            src_ref=vel_hbm.at[:, :, pl.ds(cells - BLK, BLK)],
            dst_ref=mirror,
            send_sem=fold_sem.at[0],
            recv_sem=fold_sem.at[1],
            device_id=(s, n - 1 - t),
            device_id_type=MESH,
        )

    @pl.when(s == ns - 1)
    def _():
        fold_copy().start()

    def eo_copy(i):
        return pltpu.make_async_copy(eofs_hbm.at[:, i], eo.at[i], eo_sem.at[i])

    def start_eo(i, carry):
        eo_copy(i).start()
        return carry

    id_copies, tx = {}, {}
    for m in order:
        id_copies[m] = pltpu.make_async_remote_copy(
            src_ref=ids.at[peer[m]],
            dst_ref=rids.at[m],
            send_sem=idtx_sem.at[m],
            recv_sem=idrx_sem.at[m],
            device_id=(s, peer[m]),
            device_id_type=MESH,
        )
        id_copies[m].start()

    @pl.when(s == ns - 1)
    def _():
        fold_copy().wait()
        flip = (
            lax.broadcasted_iota(jnp.int32, (BLK, BLK), 0)
            + lax.broadcasted_iota(jnp.int32, (BLK, BLK), 1)
            == BLK - 1
        )
        flip = jnp.where(flip, 1.0, 0.0).astype(jnp.bfloat16)
        parts = []
        for comp in range(comps):
            flipped = jnp.dot(mirror[comp], flip, preferred_element_type=jnp.float32)
            own = vel[comp, :, cells - BLK : cells].astype(jnp.float32)
            parts.append(0.5 * (own - flipped))
        c, d = cs[sb - 1 : sb, :], sn[sb - 1 : sb, :]
        x, y = parts
        rot[sb - 1, 0:rows, :] = (c * x - d * y).astype(jnp.bfloat16)
        rot[sb - 1, rows:both, :] = (d * x + c * y).astype(jnp.bfloat16)

    def contribute(k, m, dest):
        p = xor_of(t, m, n)
        w_copies[k].wait()

        def slot(j, carry):
            block = rot[sblk_ref[p, j]]
            value = jnp.dot(block, w[m, j], preferred_element_type=jnp.float32)
            dest[m, j] = value.astype(jnp.bfloat16)
            return carry

        lax.fori_loop(0, cap, slot, 0, unroll=4)

    def send_copy(m):
        return pltpu.make_async_remote_copy(
            src_ref=send.at[m],
            dst_ref=recv.at[m],
            send_sem=tx_sem.at[m],
            recv_sem=rx_sem.at[m],
            device_id=(s, xor_of(t, m, n)),
            device_id_type=MESH,
        )

    for k, m in enumerate(order):
        contribute(k, m, send)
        send_copy(m).start()
    lax.fori_loop(0, nt, start_eo, 0)
    contribute(n - 1, 0, recv)

    def stage(i, carry):
        eo_copy(i).wait()
        lanes = pl.ds(pl.multiple_of(i * BLK, BLK), BLK)
        flat[:, lanes] = eo[i].reshape(flat.shape[0], BLK)
        return carry

    lax.fori_loop(0, nt, stage, 0)

    diagonal = (
        lax.broadcasted_iota(jnp.int32, (group, BLK), 1) % group
        == lax.broadcasted_iota(jnp.int32, (group, BLK), 0)
    )

    def place(m, tile):
        wide = jnp.concatenate([tile] * (group // 8), axis=0)

        def per_block(b, carry):
            hit = jnp.where((wide == b) & diagonal, 1.0, 0.0).astype(jnp.bfloat16)
            kron[pl.ds(pl.multiple_of(b * group, group), group), m * BLK : (m + 1) * BLK] = hit
            return carry

        lax.fori_loop(0, tb, per_block, 0, unroll=4)

    place(0, ids[t])
    for m in order:
        id_copies[m].wait()
        place(m, rids[m])
    for m in order:
        send_copy(m).wait()
    for r in range(0, both, group):
        right = recv[:, :, r : r + group, :].reshape(n * cap * group, BLK)
        summed = jnp.dot(kron[...], right, preferred_element_type=jnp.float32)
        for b in range(tb):
            rem[r : r + group, b * BLK : (b + 1) * BLK] = summed[
                b * group : (b + 1) * group, :
            ].astype(jnp.bfloat16)
    out_copies = []
    for comp in range(comps):
        copy = pltpu.make_async_copy(
            rem.at[pl.ds(comp * rows, rows), :], out_hbm.at[comp], out_sem.at[comp]
        )
        copy.start()
        out_copies.append(copy)

    kk = eo.shape[1]

    chunk = min(256, comps * kk)

    def product(i, carry):
        at = pl.ds(pl.multiple_of(i * chunk, chunk), chunk)
        res[at, 0:both] = lax.dot_general(
            flat[at, :], rem[...], NT_DIMS, preferred_element_type=jnp.float32
        )
        return carry

    lax.fori_loop(0, comps * kk // chunk, product, 0)
    kb = kk // n
    half = kb // 2
    for d in range(n):
        for h in range(2):
            base = comps * (d * kb + h * half)
            first = res[pl.ds(base, half, stride=2), :]
            second = res[pl.ds(base + 1, half, stride=2), :]
            part = first[:, 0:rows] + second[:, rows:both]
            piece[d, :, h * rows : (h + 1) * rows] = part.astype(piece.dtype)

    ptx = []
    for m in order:
        copy = pltpu.make_async_remote_copy(
            src_ref=piece.at[peer[m]],
            dst_ref=rpiece.at[m],
            send_sem=ptx_sem.at[m],
            recv_sem=prx_sem.at[m],
            device_id=(s, peer[m]),
            device_id_type=MESH,
        )
        copy.start()
        ptx.append(copy)
    for copy in ptx:
        copy.wait()
    total = piece[t].astype(jnp.float32)
    for m in order:
        total = total + rpiece[m].astype(jnp.float32)
    rq[s] = total
    qtx = []
    for i in range(1, ns):
        copy = pltpu.make_async_remote_copy(
            src_ref=rq.at[s],
            dst_ref=rq.at[s],
            send_sem=qtx_sem.at[i],
            recv_sem=qrx_sem.at[i],
            device_id=((s + i) % ns, t),
            device_id_type=MESH,
        )
        copy.start()
        qtx.append(copy)
    for copy in qtx:
        copy.wait()
    final = rq[0]
    for i in range(1, ns):
        final = final + rq[i]
    final = jnp.concatenate([final[:, 0:rows], final[:, rows:both]], axis=0)
    pcs_ref[...] = final.T
    for copy in out_copies:
        copy.wait()


def per_device(n, ns, src_vel, angle, src_block, tgt_block, send_count, intersection, eofs):
    comps, rows, cells = src_vel.shape
    cap = src_block.shape[3]
    kk, _, tcells = eofs.shape
    tb, nt, sb = tcells // BLK, tcells // BLK, cells // BLK
    eo = eofs.reshape(kk, comps, nt, BLK).transpose(0, 2, 1, 3)
    both = comps * rows
    kb = kk // n
    bf, f32 = jnp.bfloat16, jnp.float32
    vmem, dma = pltpu.VMEM, pltpu.SemaphoreType.DMA
    anyspace = pl.BlockSpec(memory_space=pl.ANY)
    scalars = pl.BlockSpec(memory_space=pltpu.SMEM)
    inside = pl.BlockSpec(memory_space=pltpu.VMEM)
    remapped, pcs = pl.pallas_call(
        functools.partial(kernel, n, ns),
        out_shape=(
            jax.ShapeDtypeStruct((comps, rows, tcells), bf),
            jax.ShapeDtypeStruct((rows, kb), f32),
        ),
        in_specs=[
            anyspace, inside, scalars, scalars, scalars, anyspace, anyspace,
        ],
        out_specs=(anyspace, inside),
        scratch_shapes=[
            vmem((comps, rows, cells), bf),
            vmem((n, cap, BLK, BLK), bf),
            vmem((nt, kk, comps, BLK), bf),
            vmem((comps * kk, tcells), bf),
            vmem((comps, rows, BLK), bf),
            vmem((sb, BLK), f32),
            vmem((sb, BLK), f32),
            vmem((sb, both, BLK), bf),
            vmem((n, cap, both, BLK), bf),
            vmem((n, cap, both, BLK), bf),
            vmem((n, 8, BLK), jnp.int32),
            vmem((n, 8, BLK), jnp.int32),
            vmem((tb * (BLK // cap), n * BLK), bf),
            vmem((both, tcells), bf),
            vmem((comps * kk, BLK), f32),
            vmem((n, kb // 2, BLK), bf),
            vmem((n, kb // 2, BLK), bf),
            vmem((ns, kb // 2, BLK), f32),
            dma, dma((n,)), dma((nt,)), dma((2,)), dma((n,)), dma((n,)), dma((n,)), dma((n,)),
            dma((comps,)), dma((n,)), dma((n,)), dma((ns,)), dma((ns,)),
        ],
        compiler_params=pltpu.CompilerParams(
            collective_id=0, has_side_effects=True, vmem_limit_bytes=60 * 1024 * 1024
        ),
    )(
        src_vel,
        angle.reshape(sb, BLK),
        src_block.reshape(n, cap),
        tgt_block.reshape(n, cap),
        send_count.reshape(n),
        intersection.reshape(n, cap, BLK, BLK),
        eo,
    )
    return remapped, pcs


def solution(mesh):
    return jax.shard_map(
        functools.partial(per_device, mesh.shape["tgt"], mesh.shape["src"]),
        mesh=mesh,
        in_specs=(
            P(None, None, ("src", "tgt")),
            P(("src", "tgt")),
            P("src", "tgt", None, None),
            P("src", "tgt", None, None),
            P("src", "tgt", None),
            P("src", "tgt", None, None, None, None),
            P(None, None, ("src", "tgt")),
        ),
        out_specs=(P(None, None, ("src", "tgt")), P(None, "tgt")),
        check_vma=False,
    )
```

profile of v0, /device:TPU:0, one launch (start us, length us, event | category | flops | bytes accessed | tf_op | source)
XLA Modules:
  0.0 61.1 jit_solution(8769759312693627447)
XLA Ops:
  0.6 57.0 %shard_map.86 = (bf16[2,48,4096]{2,1,0:T(8,128)(2,1)}, f32[48,64]{1,0:T(8,128)}) custom-call(bf16[2,48,4096]{2,1,0:T(8,128)(2,1)} %vel_hbm.1, f32[32,128]{1,0:T(8,128)} %bitcast.10, s32[8,8]{1,0:T(8,128)} %bitcast.11, s32[8,8]{1,0:T(8,128)} %bitcast.12, s32[8]{0:T(128)} %bitcast.13, bf16[8,8,128,128]{3,2,1,0:T(8,128)(2,1)} %bitcast.9, ...), custom_call_target="tpu_custom_call" | custom-call | tf_op jit(solution)/shard_map/pallas_call | solution.py:281
  57.6 2.1 %copy.11 = bf16[2,48,4096]{2,1,0:T(8,128)(2,1)} copy(bf16[2,48,4096]{2,1,0:T(8,128)(2,1)} %get-tuple-element.4) | data formatting | bytes 1572864
  59.7 1.3 %copy.12 = f32[48,64]{1,0:T(8,128)} copy(f32[48,64]{1,0:T(8,128)} %get-tuple-element.5) | data formatting | bytes 24576
where the time goes:
time: 61.4 us; the launch traced here: 61.1 us
  Pallas kernels  57 us (93%)
  local copies, waits for them, and re-layouts  3.41 us (6%)
  between operations  0.64 us (1%)
    pallas_call x1, Pallas kernels, per_device(): pl.pallas_call(functools.partial(kernel, n, ns), out_shape=(jax.ShapeDtyp...  57 us
    unnamed x2, local copies, waits for them, and re-layouts  3.41 us

commit v1 on v0

v1 whole, which is shorter than its diff:
```python
import functools

import jax
import jax.numpy as jnp
from jax import lax
from jax.experimental import pallas as pl
from jax.experimental.pallas import tpu as pltpu
from jax.sharding import PartitionSpec as P

BLK = 128
PARTS = 2
MESH = pl.DeviceIdType.MESH
NT_DIMS = (((1,), (1,)), ((), ()))


def xor_of(index, mask, count):
    result, bit = 0, 1
    while bit < count:
        result = result + (((index // bit) + (mask // bit)) % 2) * bit
        bit *= 2
    return result


def send_orders(n, nx):
    nz = n // nx
    zs = list(range(1, nz))
    near, far = [z for z in zs if z < nz // 2], [z for z in zs if z >= nz // 2]
    far = far[::-1]

    def masks(steps):
        return [z * nx + x for z in steps for x in range(nx)]

    line = list(range(1, nx))
    inner = masks(far[:1]) + masks(near) + line + masks(far[1:])
    outer = masks(near) + line + masks(far)
    waits = line + masks(near) + masks(far)
    return inner, outer, waits


def kernel(
    n, ns, vel_hbm, angle_hbm, sblk_hbm, tblk_hbm, count_hbm, w_hbm, eofs_hbm,
    out_ref, pcs_ref,
    angle_ref, sblk_ref, tblk_ref, count_ref, vel, w, eo, flat, mirror, cs, sn, rot, send, recv, ids, rids, sids, kron, res, piece, rpiece, rq,
    in_sem, vel_sem, w_sem, eo_sem, fold_sem, tx_sem, rx_sem, idtx_sem, idrx_sem, ids_sem,
    ptx_sem, prx_sem, qtx_sem, qrx_sem,
):
    s, t = lax.axis_index("src"), lax.axis_index("tgt")
    comps, rows, cells = vel.shape
    sb = cells // BLK
    cap = w.shape[1]
    nt, kk2 = flat.shape[0], flat.shape[1]
    tb = nt
    group = BLK // cap
    both = comps * rows
    nx = max(1, ns // 2)
    nz = n // nx
    z = t // nx
    outer = jnp.logical_or(z == 0, z == nz - 1)
    inner_order, outer_order, waits = send_orders(n, nx)
    order = [jnp.where(outer, b, a) for a, b in zip(inner_order, outer_order)] + [0]
    everyone = list(range(1, n))
    peer = {m: xor_of(t, m, n) for m in range(n)}

    vel_copy = pltpu.make_async_copy(vel_hbm, vel, vel_sem)
    vel_copy.start()
    small = [
        pltpu.make_async_copy(angle_hbm, angle_ref, in_sem.at[0]),
        pltpu.make_async_copy(tblk_hbm, tblk_ref, in_sem.at[1]),
        pltpu.make_async_copy(sblk_hbm, sblk_ref, in_sem.at[2]),
        pltpu.make_async_copy(count_hbm, count_ref, in_sem.at[3]),
    ]
    for copy in small:
        copy.start()

    def w_copy(k):
        return pltpu.make_async_copy(w_hbm.at[xor_of(t, order[k], n)], w.at[k], w_sem.at[k])

    for k in range(n):
        w_copy(k).start()

    barrier = pltpu.get_barrier_semaphore()
    for m in everyone:
        pl.semaphore_signal(barrier, inc=1, device_id=(s, peer[m]), device_id_type=MESH)
    for i in range(1, ns):
        pl.semaphore_signal(barrier, inc=1, device_id=((s + i) % ns, t), device_id_type=MESH)

    for copy in small:
        copy.wait()
    cs[...] = jnp.cos(angle_ref[...])
    sn[...] = jnp.sin(angle_ref[...])
    lane_slot = lax.broadcasted_iota(jnp.int32, (8, BLK), 1) // group

    def own_ids(p, carry):
        tile = jnp.zeros((8, BLK), jnp.int32)
        for j in range(cap):
            tile = jnp.where(lane_slot == j, tblk_ref[p, j], tile)
        ids[p] = tile
        return carry

    lax.fori_loop(0, n, own_ids, 0)
    vel_copy.wait()

    def rotate(b, carry):
        lanes = pl.ds(pl.multiple_of(b * BLK, BLK), BLK)
        c, d = cs[pl.ds(b, 1), :], sn[pl.ds(b, 1), :]
        x = vel[0, :, lanes].astype(jnp.float32)
        y = vel[1, :, lanes].astype(jnp.float32)
        rot[b, 0:rows, :] = (c * x - d * y).astype(jnp.bfloat16)
        rot[b, rows:both, :] = (d * x + c * y).astype(jnp.bfloat16)
        return carry

    lax.fori_loop(0, sb, rotate, 0, unroll=2)
    pl.semaphore_wait(barrier, n - 1 + ns - 1)

    def fold_copy():
        return pltpu.make_async_remote_copy(
            src_ref=vel_hbm.at[:, :, pl.ds(cells - BLK, BLK)],
            dst_ref=mirror,
            send_sem=fold_sem.at[0],
            recv_sem=fold_sem.at[1],
            device_id=(s, n - 1 - t),
            device_id_type=MESH,
        )

    @pl.when(s == ns - 1)
    def _():
        fold_copy().start()

    id_copies = {}
    for m in everyone:
        id_copies[m] = pltpu.make_async_remote_copy(
            src_ref=ids.at[peer[m]],
            dst_ref=rids.at[m],
            send_sem=idtx_sem.at[m],
            recv_sem=idrx_sem.at[m],
            device_id=(s, peer[m]),
            device_id_type=MESH,
        )
        id_copies[m].start()

    @pl.when(s == ns - 1)
    def _():
        fold_copy().wait()
        flip = (
            lax.broadcasted_iota(jnp.int32, (BLK, BLK), 0)
            + lax.broadcasted_iota(jnp.int32, (BLK, BLK), 1)
            == BLK - 1
        )
        flip = jnp.where(flip, 1.0, 0.0).astype(jnp.bfloat16)
        parts = []
        for comp in range(comps):
            flipped = jnp.dot(mirror[comp], flip, preferred_element_type=jnp.float32)
            own = vel[comp, :, cells - BLK : cells].astype(jnp.float32)
            parts.append(0.5 * (own - flipped))
        c, d = cs[sb - 1 : sb, :], sn[sb - 1 : sb, :]
        x, y = parts
        rot[sb - 1, 0:rows, :] = (c * x - d * y).astype(jnp.bfloat16)
        rot[sb - 1, rows:both, :] = (d * x + c * y).astype(jnp.bfloat16)

    span = cap // PARTS

    def contribute(k, h, dest, at):
        p = xor_of(t, order[k], n)

        def slot(i, carry):
            j = h * span + i
            block = rot[sblk_ref[p, j]]
            value = jnp.dot(block, w[k, j], preferred_element_type=jnp.float32)
            value = jnp.where(j < count_ref[p], value, 0.0)
            dest[at, j] = value.astype(jnp.bfloat16)
            return carry

        lax.fori_loop(0, span, slot, 0, unroll=True)

    def send_copy(k, m, h):
        part = pl.ds(h * span, span)
        return pltpu.make_async_remote_copy(
            src_ref=send.at[k, part],
            dst_ref=recv.at[m, part],
            send_sem=tx_sem.at[k, h],
            recv_sem=rx_sem.at[m, h],
            device_id=(s, xor_of(t, m, n)),
            device_id_type=MESH,
        )

    for k in range(n - 1):
        w_copy(k).wait()
        for h in range(PARTS):
            contribute(k, h, send, k)
            send_copy(k, order[k], h).start()

    def eo_copy(i):
        return pltpu.make_async_copy(eofs_hbm.at[:, i], eo.at[i], eo_sem.at[i])

    def start_eo(i, carry):
        eo_copy(i).start()
        return carry

    lax.fori_loop(0, nt, start_eo, 0)
    w_copy(n - 1).wait()
    for h in range(PARTS):
        contribute(n - 1, h, recv, 0)

    def stage(i, carry):
        eo_copy(i).wait()
        flat[i] = eo[i].reshape(kk2, BLK)
        return carry

    lax.fori_loop(0, nt, stage, 0)

    diagonal = (
        lax.broadcasted_iota(jnp.int32, (group, BLK), 1) % group
        == lax.broadcasted_iota(jnp.int32, (group, BLK), 0)
    )

    def place(m, tile):
        wide = jnp.concatenate([tile] * (group // 8), axis=0)

        def per_block(b, carry):
            hit = jnp.where((wide == b) & diagonal, 1.0, 0.0).astype(jnp.bfloat16)
            kron[pl.ds(pl.multiple_of(b * group, group), group), m * BLK : (m + 1) * BLK] = hit
            return carry

        lax.fori_loop(0, tb, per_block, 0, unroll=4)

    place(0, ids[t])
    to_scalars = {}
    for m in everyone:
        id_copies[m].wait()
        to_scalars[m] = pltpu.make_async_copy(rids.at[m], sids.at[m], ids_sem.at[m])
        to_scalars[m].start()
        place(m, rids[m])
    for m in everyone:
        to_scalars[m].wait()

    chunk = min(512, kk2)

    def product(m, h, first):
        slots = range(h * span, (h + 1) * span)
        blocks = [tblk_ref[t, j] if m == 0 else sids[m, 0, j * group] for j in slots]
        right = jnp.concatenate([recv[m, j] for j in slots], axis=1)

        def piece_of(i, carry):
            at = pl.ds(pl.multiple_of(i * chunk, chunk), chunk)
            left = jnp.concatenate([flat[b, at, :] for b in blocks], axis=1)
            value = lax.dot_general(left, right, NT_DIMS, preferred_element_type=jnp.float32)
            res[at, 0:both] = value if first else res[at, 0:both] + value
            return carry

        lax.fori_loop(0, kk2 // chunk, piece_of, 0)

    for h in range(PARTS):
        product(0, h, h == 0)
    for m in waits:
        for h in range(PARTS):
            send_copy(0, m, h).wait_recv()
            product(m, h, False)

    kb = kk2 // comps // n
    half = kb // 2
    for d in range(n):
        for h in range(2):
            base = comps * (d * kb + h * half)
            first = res[pl.ds(base, half, stride=2), :]
            second = res[pl.ds(base + 1, half, stride=2), :]
            part = first[:, 0:rows] + second[:, rows:both]
            piece[d, :, h * rows : (h + 1) * rows] = part.astype(piece.dtype)

    ptx = []
    for m in everyone[::-1]:
        copy = pltpu.make_async_remote_copy(
            src_ref=piece.at[peer[m]],
            dst_ref=rpiece.at[m],
            send_sem=ptx_sem.at[m],
            recv_sem=prx_sem.at[m],
            device_id=(s, peer[m]),
            device_id_type=MESH,
        )
        copy.start()
        ptx.append(copy)

    for r in range(0, both, group):
        right = recv[:, :, r : r + group, :].reshape(n * cap * group, BLK)
        summed = jnp.dot(kron[...], right, preferred_element_type=jnp.float32)
        comp, row = r // rows, r % rows
        for b in range(tb):
            out_ref[comp, row : row + group, b * BLK : (b + 1) * BLK] = summed[
                b * group : (b + 1) * group, :
            ].astype(jnp.bfloat16)

    for copy in ptx:
        copy.wait()
    total = piece[t].astype(jnp.float32)
    for m in everyone:
        total = total + rpiece[m].astype(jnp.float32)
    rq[s] = total
    qtx = []
    for i in range(1, ns):
        copy = pltpu.make_async_remote_copy(
            src_ref=rq.at[s],
            dst_ref=rq.at[s],
            send_sem=qtx_sem.at[i],
            recv_sem=qrx_sem.at[i],
            device_id=((s + i) % ns, t),
            device_id_type=MESH,
        )
        copy.start()
        qtx.append(copy)
    for copy in qtx:
        copy.wait()
    final = rq[0]
    for i in range(1, ns):
        final = final + rq[i]
    final = jnp.concatenate([final[:, 0:rows], final[:, rows:both]], axis=0)
    pcs_ref[...] = final.T
    for k in range(n - 1):
        for h in range(PARTS):
            send_copy(k, order[k], h).wait_send()


def per_device(n, ns, src_vel, angle, src_block, tgt_block, send_count, intersection, eofs):
    comps, rows, cells = src_vel.shape
    cap = src_block.shape[3]
    kk, _, tcells = eofs.shape
    tb, nt, sb = tcells // BLK, tcells // BLK, cells // BLK
    eo = eofs.reshape(kk, comps, nt, BLK).transpose(0, 2, 1, 3)
    both = comps * rows
    kb = kk // n
    bf, f32 = jnp.bfloat16, jnp.float32
    vmem, dma = pltpu.VMEM, pltpu.SemaphoreType.DMA
    outside = pl.BlockSpec(memory_space=pltpu.HBM)
    smem = pltpu.SMEM
    inside = pl.BlockSpec(memory_space=pltpu.VMEM)
    remapped, pcs = pl.pallas_call(
        functools.partial(kernel, n, ns),
        out_shape=(
            jax.ShapeDtypeStruct((comps, rows, tcells), bf),
            jax.ShapeDtypeStruct((rows, kb), f32),
        ),
        in_specs=[
            outside, outside, outside, outside, outside, outside, outside,
        ],
        out_specs=(inside, inside),
        scratch_shapes=[
            vmem((sb, BLK), f32),
            smem((n, cap), jnp.int32),
            smem((n, cap), jnp.int32),
            smem((n,), jnp.int32),
            vmem((comps, rows, cells), bf),
            vmem((n, cap, BLK, BLK), bf),
            vmem((nt, kk, comps, BLK), bf),
            vmem((nt, comps * kk, BLK), bf),
            vmem((comps, rows, BLK), bf),
            vmem((sb, BLK), f32),
            vmem((sb, BLK), f32),
            vmem((sb, both, BLK), bf),
            vmem((n - 1, cap, both, BLK), bf),
            vmem((n, cap, both, BLK), bf),
            vmem((n, 8, BLK), jnp.int32),
            vmem((n, 8, BLK), jnp.int32),
            smem((n, 8, BLK), jnp.int32),
            vmem((tb * (BLK // cap), n * BLK), bf),
            vmem((comps * kk, BLK), f32),
            vmem((n, kb // 2, BLK), bf),
            vmem((n, kb // 2, BLK), bf),
            vmem((ns, kb // 2, BLK), f32),
            dma((4,)), dma, dma((n,)), dma((nt,)), dma((2,)), dma((n, PARTS)), dma((n, PARTS)), dma((n,)), dma((n,)),
            dma((n,)), dma((n,)), dma((n,)), dma((ns,)), dma((ns,)),
        ],
        compiler_params=pltpu.CompilerParams(
            collective_id=0, has_side_effects=True, vmem_limit_bytes=44 * 1024 * 1024
        ),
    )(
        *(
            pltpu.with_memory_space_constraint(value, pltpu.HBM)
            for value in (
                src_vel,
                angle.reshape(sb, BLK),
                src_block.reshape(n, cap),
                tgt_block.reshape(n, cap),
                send_count.reshape(n),
                intersection.reshape(n, cap, BLK, BLK),
                eo,
            )
        )
    )
    return remapped, pcs


def solution(mesh):
    return jax.shard_map(
        functools.partial(per_device, mesh.shape["tgt"], mesh.shape["src"]),
        mesh=mesh,
        in_specs=(
            P(None, None, ("src", "tgt")),
            P(("src", "tgt")),
            P("src", "tgt", None, None),
            P("src", "tgt", None, None),
            P("src", "tgt", None),
            P("src", "tgt", None, None, None, None),
            P(None, None, ("src", "tgt")),
        ),
        out_specs=(P(None, None, ("src", "tgt")), P(None, "tgt")),
        check_vma=False,
    )
```

time: 61.4 us -> 54.7 us (0.89)
  Pallas kernels: 57 us -> 52.4 us
  local copies, waits for them, and re-layouts: 3.41 us -> 1.49 us
    pallas_call x1, Pallas kernels: 57 us -> 52.4 us  [per_device(): pl.pallas_call(functools.partial(kernel, n, ns), out_shape=(jax.ShapeDtyp...]
    unnamed x2, local copies, waits for them, and re-layouts: 3.41 us -> 1.49 us
where the time goes in v1:
time: 54.7 us; the launch traced here: 54.5 us
  Pallas kernels  52.4 us (96%)
  local copies, waits for them, and re-layouts  1.49 us (3%)
  between operations  0.64 us (1%)
    pallas_call x1, Pallas kernels, per_device(): pl.pallas_call(functools.partial(kernel, n, ns), out_shape=(jax.ShapeDtyp...  52.4 us
    unnamed x2, local copies, waits for them, and re-layouts  1.49 us

profile of v1, /device:TPU:0, one launch (start us, length us, event | category | flops | bytes accessed | tf_op | source)
XLA Modules:
  0.0 54.5 jit_solution(17133577678826663595)
XLA Ops:
  0.6 52.4 %shard_map.86 = (bf16[2,48,4096]{2,1,0:T(8,128)(2,1)S(1)}, f32[48,64]{1,0:T(8,128)S(1)}) custom-call(bf16[2,48,4096]{2,1,0:T(8,128)(2,1)} %vel_hbm.1, f32[32,128]{1,0:T(8,128)} %bitcast.10, s32[8,8]{1,0:T(8,128)} %bitcast.11, s32[8,8]{1,0:T(8,128)} %bitcast.12, s32[8]{0:T(128)} %bitcast.13, bf16[8,8,128,128]{3,2,1,0:T(8,128)(2,1)} %bitcast.9, ...), custom_call_target="tpu_custom_call" | custom-call | tf_op jit(solution)/shard_map/pallas_call | solution.py:334
  53.0 0.9 %copy.11 = bf16[2,48,4096]{2,1,0:T(8,128)(2,1)} copy(bf16[2,48,4096]{2,1,0:T(8,128)(2,1)S(1)} %get-tuple-element.4) | data formatting | bytes 1572864
  53.9 0.6 %copy.12 = f32[48,64]{1,0:T(8,128)} copy(f32[48,64]{1,0:T(8,128)S(1)} %get-tuple-element.5) | data formatting | bytes 24576
